TPU v7x, 32 devices: a whole 2x2x4 slice. The times are simulated.
32 devices in a mesh: seq: 8 (over y, x, core), batch: 4 (over z).
Axes of the slice: x: 2, y: 2, z: 4, core: 2. Of those that a mesh axis runs over, the one named last changes fastest.
Arguments:
- tokens: bfloat16 [4, 4096, 2048], P('batch', 'seq'), may hold values from -6 to 6
- w_qkv: bfloat16 [2048, 3072], replicated, may hold values from -0.125 to 0.125
- cotangent: bfloat16 [4, 4096, 1024], P('batch', 'seq'), may hold values from -6 to 6
Outputs:
- attended: bfloat16 [4, 4096, 1024], P('batch', 'seq')
- token_grad: bfloat16 [4, 4096, 2048], P('batch', 'seq')
- weight_grad: float32 [2048, 3072], P('seq')
All inputs are finite; a program needn't handle non-finite values.
Results may differ from a plain program's by a relative error of at most 0.0064.
Values sent between devices are 32-bit elements; how exact they have to be, the bound alone decides.
A program may use at most 192 MiB of HBM per device.

v0:
```python
import jax
import jax.numpy as jnp
from jax import lax
from jax.sharding import PartitionSpec as P

HEADS = 8
DH = 128
BLK = 512
PRECISE = lax.Precision.HIGHEST


def running_states(block_states, incoming, reverse):
    zero_block = jnp.zeros_like(block_states)
    if reverse:
        totals = jnp.cumsum(block_states[::-1], axis=0)[::-1]
        return incoming[None] + jnp.concatenate([totals[1:], zero_block], 0)
    totals = jnp.cumsum(block_states, axis=0)
    return incoming[None] + jnp.concatenate([zero_block, totals[:-1]], 0)


def body(tokens, w_qkv, cotangent):
    row_count = tokens.shape[1]
    width = w_qkv.shape[1] // 3
    block_count = row_count // BLK
    seq_count = lax.axis_size("seq")
    batch_count = lax.axis_size("batch")
    local_x = tokens[0]
    projected = jnp.dot(local_x, w_qkv, preferred_element_type=jnp.float32).astype(jnp.bfloat16)
    queries = projected[:, :width].reshape(block_count, BLK, HEADS, DH)
    key_heads = projected[:, width : 2 * width].reshape(block_count, BLK, HEADS, DH)
    value_heads = projected[:, 2 * width :].reshape(block_count, BLK, HEADS, DH)
    position = lax.axis_index("seq") * row_count + jnp.arange(row_count, dtype=jnp.int32)
    pos_scale = DH ** (-0.5) / jnp.sqrt(position.astype(jnp.float32) + 1.0)
    scaled_grad = (cotangent[0].astype(jnp.float32) * pos_scale[:, None]).astype(jnp.bfloat16)
    grad_heads = scaled_grad.reshape(block_count, BLK, HEADS, DH)
    kv_blocks = jnp.einsum(
        "nrha,nrhb->nhab", key_heads, value_heads, preferred_element_type=jnp.float32
    )
    grad_blocks = jnp.einsum(
        "nrha,nrhb->nhab", queries, grad_heads, preferred_element_type=jnp.float32
    )
    kv_local = jnp.sum(kv_blocks, 0)
    grad_local = jnp.sum(grad_blocks, 0)
    kv_all, grad_all = (
        lax.all_gather(kv_local[None], "seq", axis=0, tiled=True),
        lax.all_gather(grad_local[None], "seq", axis=0, tiled=True),
    )
    rank_list = jnp.arange(seq_count, dtype=jnp.int32)
    my_rank = lax.axis_index("seq")
    kv_in = jnp.sum(jnp.where((rank_list < my_rank)[:, None, None, None], kv_all, 0.0), 0)
    grad_in = jnp.sum(jnp.where((rank_list > my_rank)[:, None, None, None], grad_all, 0.0), 0)
    kv_before = running_states(kv_blocks, kv_in, False)
    grad_after = running_states(grad_blocks, grad_in, True)
    causal = jnp.arange(BLK)[:, None] >= jnp.arange(BLK)[None, :]
    scores = jnp.where(
        causal,
        jnp.einsum("nihd,njhd->nhij", queries, key_heads, preferred_element_type=jnp.float32),
        0.0,
    ).astype(jnp.bfloat16)
    grad_scores = jnp.where(
        causal,
        jnp.einsum("nihd,njhd->nhij", grad_heads, value_heads, preferred_element_type=jnp.float32),
        0.0,
    ).astype(jnp.bfloat16)
    query_wide = queries.astype(jnp.float32)
    key_wide = key_heads.astype(jnp.float32)
    value_wide = value_heads.astype(jnp.float32)
    grad_wide = grad_heads.astype(jnp.float32)
    attended = jnp.einsum(
        "nhij,njhd->nihd", scores, value_heads, preferred_element_type=jnp.float32
    )
    attended = attended + jnp.einsum("nihd,nhde->nihe", query_wide, kv_before, precision=PRECISE)
    attended = attended * pos_scale.reshape(block_count, BLK, 1, 1)
    query_grad = jnp.einsum(
        "nhij,njhd->nihd", grad_scores, key_heads, preferred_element_type=jnp.float32
    )
    query_grad = query_grad + jnp.einsum("nihe,nhde->nihd", grad_wide, kv_before, precision=PRECISE)
    key_grad = jnp.einsum(
        "nhij,nihd->njhd", grad_scores, queries, preferred_element_type=jnp.float32
    )
    key_grad = key_grad + jnp.einsum("njhe,nhde->njhd", value_wide, grad_after, precision=PRECISE)
    value_grad = jnp.einsum(
        "nhij,nihe->njhe", scores, grad_heads, preferred_element_type=jnp.float32
    )
    value_grad = value_grad + jnp.einsum("njhd,nhde->njhe", key_wide, grad_after, precision=PRECISE)
    qkv_grad = jnp.concatenate(
        [
            query_grad.reshape(row_count, width),
            key_grad.reshape(row_count, width),
            value_grad.reshape(row_count, width),
        ],
        1,
    ).astype(jnp.bfloat16)
    token_grad = lax.dot_general(
        qkv_grad, w_qkv, (((1,), (1,)), ((), ())), preferred_element_type=jnp.float32
    )
    token_grad = token_grad.astype(jnp.bfloat16)[None]
    partial_rows = lax.psum_scatter(
        lax.dot_general(
            local_x, qkv_grad, (((0,), (0,)), ((), ())), preferred_element_type=jnp.float32
        ),
        "seq",
        scatter_dimension=0,
        tiled=True,
    )
    summed = lax.psum(partial_rows, "batch")
    grad_scale = 1.0 / jnp.sqrt(jnp.float32(batch_count * seq_count * row_count))
    weight_grad = summed * grad_scale
    return (attended.reshape(row_count, width).astype(jnp.bfloat16)[None], token_grad, weight_grad)


def solution(mesh):
    return jax.shard_map(
        body,
        mesh=mesh,
        in_specs=(P("batch", "seq", None), P(), P("batch", "seq", None)),
        out_specs=(P("batch", "seq", None), P("batch", "seq", None), P("seq", None)),
        check_vma=False,
    )
```

profile of v0, /device:TPU:0, one launch (start us, length us, event | category | flops | bytes accessed | tf_op | source)
XLA Modules:
  0.0 420.3 jit_solution(13077857208843234971)
XLA Ops:
  7.2 2.7 copy.51
  10.0 9.6 %convolution_convert_fusion = bf16[512,3072]{1,0:T(8,128)(2,1)S(1)} fusion(bf16[2048,3072]{1,0:T(8,128)(2,1)} %param.4, bf16[1,512,2048]{2,1,0:T(8,128)(2,1)S(1)} %copy-done), kind=kOutput, calls=%fused_computation.3 | convolution fusion | flops 6444023808 | bytes 17825792 | tf_op jit(solution)/shard_map/dot_general | solution.py:28
  19.6 2.2 slice_bitcast_fusion.2
  21.8 2.3 copy.52
  28.4 2.5 copy.55
  30.9 2.4 copy.29
  33.3 2.5 fusion.10
  36.1 2.8 select_convert_fusion
  40.4 2.0 fusion.21
  42.5 2.9 fusion.20
  45.4 2.0 fusion.23
  47.4 20.4 %all-gather.7.cloned.1.call-done = f32[64,128,128]{2,1,0:T(8,128)} async-done(((f32[8,128,128]{2,1,0:T(8,128)}), f32[64,128,128]{2,1,0:T(8,128)}) %all-gather.7.cloned.1.call-update) | async-done | bytes 4194320 | tf_op jit(solution)/shard_map/all_gather | solution.py:46
  67.8 2.9 select_reduce_fusion
  70.9 2.2 add_convert_fusion
  73.1 2.1 add_convert_fusion.1
  75.2 31.1 %all-gather.5.cloned.1.call-done = f32[64,128,128]{2,1,0:T(8,128)} async-done(((f32[8,128,128]{2,1,0:T(8,128)}), f32[64,128,128]{2,1,0:T(8,128)}) %all-gather.5.cloned.1.call-update) | async-done | bytes 4194320 | tf_op jit(solution)/shard_map/all_gather | solution.py:45
  106.3 2.9 select_reduce_fusion.1
  111.6 15.2 %convolution_bitcast_fusion = f32[2048,3072]{0,1:T(8,128)} fusion(bf16[1,512,2048]{2,1,0:T(8,128)(2,1)S(1)} %copy-done, bf16[512,1024]{0,1:T(8,128)(2,1)S(1)} %bitcast.86, bf16[512,1024]{0,1:T(8,128)(2,1)S(1)} %bitcast.88, bf16[512,1024]{0,1:T(8,128)(2,1)S(1)} %bitcast.89), kind=kOutput, calls=%fused_computation | convolution fusion | flops 6451888128 | bytes 30408704 | tf_op jit(solution)/shard_map/dot_general | solution.py:99
  126.9 156.1 %reduce-scatter.2.cloned.1.call-done = f32[256,3072]{0,1:T(8,128)} async-done(((f32[2048,3072]{0,1:T(8,128)}), f32[256,3072]{0,1:T(8,128)}) %reduce-scatter.2.cloned.1.call-update) | async-done | bytes 3145744 | tf_op jit(solution)/shard_map/reduce_scatter | solution.py:98
  283.0 3.8 fusion.6
  289.3 13.6 %fusion = bf16[1,512,2048]{2,1,0:T(8,128)(2,1)} fusion(bf16[2048,3072]{1,0:T(8,128)(2,1)} %param.4, bf16[512,1024]{0,1:T(8,128)(2,1)} %bitcast.85, bf16[512,1024]{0,1:T(8,128)(2,1)} %bitcast.87, bf16[512,1024]{0,1:T(8,128)(2,1)} %bitcast.90), kind=kOutput, calls=%fused_computation.8 | convolution fusion | flops 6452936704 | bytes 17825792 | tf_op jit(solution)/shard_map/dot_general | solution.py:94
  302.9 103.4 %all-reduce.2.cloned.1.call-done = f32[256,3072]{0,1:T(8,128)} async-done(((f32[256,3072]{0,1:T(8,128)}), f32[256,3072]{0,1:T(8,128)}) %all-reduce.2.cloned.1.call-update) | async-done | bytes 3145744 | tf_op jit(solution)/shard_map/psum | solution.py:106
  406.3 3.9 broadcast_multiply_fusion
  410.2 3.5 copy.45
  (58 shorter events, 11.3 us)
Async XLA Ops:
  7.2 2.8 copy-start
  7.2 60.6 %all-gather.7.cloned.1.call-start = ((), (), s32[]{:S(2)}) async-start(), calls=%async_computation.4 | async-start | bytes 4718592 | tf_op jit(solution)/shard_map/all_gather | solution.py:46
  24.1 3.0 copy-start.3
  26.0 1.0 copy-start.6
  28.3 78.0 %all-gather.5.cloned.1.call-start = ((), (), s32[]{:S(2)}) async-start(), calls=%async_computation.3 | async-start | bytes 4718592 | tf_op jit(solution)/shard_map/all_gather | solution.py:45
  35.8 247.2 %reduce-scatter.2.cloned.1.call-start = ((), (), s32[]{:S(2)}) async-start(), calls=%async_computation.1 | async-start | bytes 28311552 | tf_op jit(solution)/shard_map/reduce_scatter | solution.py:98
  36.1 2.8 copy-start.4
  36.1 2.8 copy-start.15
  40.4 4.9 %copy-start.2 = (bf16[8,512,512]{2,1,0:T(8,128)(2,1)}, bf16[8,512,512]{2,1,0:T(8,128)(2,1)S(1)}, u32[]{:S(2)}) copy-start(bf16[8,512,512]{2,1,0:T(8,128)(2,1)S(1)} %select_convert_fusion.1) | copy-start | bytes 12582916
  40.4 2.0 copy-start.9
  42.5 2.9 copy-start.7
  67.8 2.9 copy-start.12
  67.8 3.1 copy-start.16
  70.9 2.2 copy-start.11
  106.3 2.9 copy-start.8
  106.3 3.2 copy-start.10
  109.5 1.2 copy-start.13
  109.5 2.1 copy-start.17
  109.5 2.1 copy-start.18
  110.7 1.0 copy-start.19
  126.8 279.5 %all-reduce.2.cloned.1.call-start = ((), (), s32[]{:S(2)}) async-start(), calls=%async_computation.2 | async-start | bytes 6291456 | tf_op jit(solution)/shard_map/psum | solution.py:106
  283.0 3.8 copy-start.5
  283.0 3.8 copy-start.14
  406.3 7.5 %copy-start.1 = (bf16[1,512,2048]{2,1,0:T(8,128)(2,1)S(1)}, bf16[1,512,2048]{2,1,0:T(8,128)(2,1)}, u32[]{:S(2)}) copy-start(bf16[1,512,2048]{2,1,0:T(8,128)(2,1)} %param.3) | copy-start | bytes 6291460
Sparse Core Ops, SparseCore 0:
  28.5 39.3 all-gather.6
  69.7 36.5 all-gather.4
  126.9 156.0 reduce-scatter.1
  285.2 121.0 all-reduce.1
where the time goes:
time: 421 us; the launch traced here: 420 us
  waiting for transfers between devices  311 us (74%)
  matrix products  63.7 us (15%)
  local copies, waits for them, and re-layouts  19.4 us (5%)
  between operations  14 us (3%)
  other arithmetic  11.8 us (3%)
    reduce_scatter x1, waiting for transfers between devices, body(): lax.psum_scatter(lax.dot_general(local_x, qkv_grad, (((0,), (0,)), ((), (...  156 us
    psum x1, waiting for transfers between devices, body(): summed = lax.psum(partial_rows, 'batch')  103 us
    all_gather x1, waiting for transfers between devices, body(): lax.all_gather(kv_local[None], 'seq', axis=0, tiled=True)  31.1 us
    all_gather x1, waiting for transfers between devices, body(): lax.all_gather(grad_local[None], 'seq', axis=0, tiled=True)  20.4 us
    dot_general x1, matrix products, body(): lax.dot_general(local_x, qkv_grad, (((0,), (0,)), ((), ())), preferred_el...  15.2 us
    dot_general x1, matrix products, body(): lax.dot_general(qkv_grad, w_qkv, (((1,), (1,)), ((), ())), preferred_elem...  13.6 us
    unnamed x44, local copies, waits for them, and re-layouts  12 us
    dot_general x1, matrix products, body(): jnp.dot(local_x, w_qkv, preferred_element_type=jnp.float32)  9.63 us
  transfers between devices with their start and end apart: 4, of which 4 were waited for; matrix products, arithmetic and copies ran while one was open for 11% of the time, Pallas kernels for 0%

commit v1 on v0

--- a/solution.py
+++ b/solution.py
@@ -103,7 +103,7 @@
         scatter_dimension=0,
         tiled=True,
     )
-    summed = lax.psum(partial_rows, "batch")
+    summed = jnp.sum(lax.all_gather(partial_rows, "batch"), axis=0)
     grad_scale = 1.0 / jnp.sqrt(jnp.float32(batch_count * seq_count * row_count))
     weight_grad = summed * grad_scale
     return (attended.reshape(row_count, width).astype(jnp.bfloat16)[None], token_grad, weight_grad)

time: 421 us -> 552 us (1.31)
  waiting for transfers between devices: 311 us -> 406 us
  other arithmetic: 11.8 us -> 31.3 us
  local copies, waits for them, and re-layouts: 19.4 us -> 35.2 us
    all_gather x0 -> x1, waiting for transfers between devices: none -> 198 us  [body(): summed = jnp.sum(lax.all_gather(partial_rows, 'batch'), axis=0)]
    psum x1 -> x0, waiting for transfers between devices: 103 us -> none  [body(): summed = lax.psum(partial_rows, 'batch')]
    reduce_sum x0 -> x1, other arithmetic: none -> 19.5 us  [body(): summed = jnp.sum(lax.all_gather(partial_rows, 'batch'), axis=0)]
    all_gather x0 -> x1, local copies, waits for them, and re-layouts: none -> 15.5 us  [body(): summed = jnp.sum(lax.all_gather(partial_rows, 'batch'), axis=0)]
  transfers between devices with their start and end apart: 4 -> 4, of which waited for: 4 -> 4; matrix products, arithmetic and copies ran while one was open for 11% -> 9% of each run, Pallas kernels for 0% -> 0%
where the time goes in v1:
time: 552 us
  waiting for transfers between devices  406 us (74%)
  matrix products  65 us (12%)
  local copies, waits for them, and re-layouts  35.2 us (6%)
  other arithmetic  31.3 us (6%)
  between operations  14 us (3%)
    all_gather x1, waiting for transfers between devices, body(): summed = jnp.sum(lax.all_gather(partial_rows, 'batch'), axis=0)  198 us
    reduce_scatter x1, waiting for transfers between devices, body(): lax.psum_scatter(lax.dot_general(local_x, qkv_grad, (((0,), (0,)), ((), (...  156 us
    all_gather x1, waiting for transfers between devices, body(): lax.all_gather(kv_local[None], 'seq', axis=0, tiled=True)  31.1 us
    all_gather x1, waiting for transfers between devices, body(): lax.all_gather(grad_local[None], 'seq', axis=0, tiled=True)  20.4 us
    reduce_sum x1, other arithmetic, body(): summed = jnp.sum(lax.all_gather(partial_rows, 'batch'), axis=0)  19.5 us
    all_gather x1, local copies, waits for them, and re-layouts, body(): summed = jnp.sum(lax.all_gather(partial_rows, 'batch'), axis=0)  15.5 us
    dot_general x1, matrix products, body(): lax.dot_general(local_x, qkv_grad, (((0,), (0,)), ((), ())), preferred_el...  15.2 us
    dot_general x1, matrix products, body(): lax.dot_general(qkv_grad, w_qkv, (((1,), (1,)), ((), ())), preferred_elem...  14.9 us
  transfers between devices with their start and end apart: 4, of which 4 were waited for; matrix products, arithmetic and copies ran while one was open for 9% of the time, Pallas kernels for 0%

profile of v1, /device:TPU:0, one launch (start us, length us, event | category | flops | bytes accessed | tf_op | source)
XLA Modules:
  0.0 551.6 jit_solution(14196115651064449253)
XLA Ops:
  7.2 2.7 copy.50
  10.0 9.6 %convolution_convert_fusion = bf16[512,3072]{1,0:T(8,128)(2,1)S(1)} fusion(bf16[2048,3072]{1,0:T(8,128)(2,1)} %param.4, bf16[1,512,2048]{2,1,0:T(8,128)(2,1)S(1)} %copy-done), kind=kOutput, calls=%fused_computation.3 | convolution fusion | flops 6444023808 | bytes 17825792 | tf_op jit(solution)/shard_map/dot_general | solution.py:28
  19.6 2.2 slice_bitcast_fusion.2
  21.8 2.3 copy.51
  28.4 2.5 copy.54
  30.9 2.4 copy.28
  33.3 2.5 fusion.10
  36.1 2.8 select_convert_fusion
  42.5 2.9 fusion.20
  47.4 20.4 %all-gather.9.cloned.1.call-done = f32[64,128,128]{2,1,0:T(8,128)} async-done(((f32[8,128,128]{2,1,0:T(8,128)}), f32[64,128,128]{2,1,0:T(8,128)}) %all-gather.9.cloned.1.call-update) | async-done | bytes 4194320 | tf_op jit(solution)/shard_map/all_gather | solution.py:46
  67.8 2.9 select_reduce_fusion
  70.9 2.2 add_convert_fusion
  73.1 2.1 add_convert_fusion.1
  75.2 31.1 %all-gather.7.cloned.1.call-done = f32[64,128,128]{2,1,0:T(8,128)} async-done(((f32[8,128,128]{2,1,0:T(8,128)}), f32[64,128,128]{2,1,0:T(8,128)}) %all-gather.7.cloned.1.call-update) | async-done | bytes 4194320 | tf_op jit(solution)/shard_map/all_gather | solution.py:45
  106.3 2.9 select_reduce_fusion.1
  111.6 15.2 %convolution_bitcast_fusion = f32[2048,3072]{0,1:T(8,128)} fusion(bf16[1,512,2048]{2,1,0:T(8,128)(2,1)S(1)} %copy-done, bf16[512,1024]{0,1:T(8,128)(2,1)S(1)} %bitcast.88, bf16[512,1024]{0,1:T(8,128)(2,1)S(1)} %bitcast.90, bf16[512,1024]{0,1:T(8,128)(2,1)S(1)} %bitcast.91), kind=kOutput, calls=%fused_computation | convolution fusion | flops 6451888128 | bytes 30408704 | tf_op jit(solution)/shard_map/dot_general | solution.py:99
  126.9 156.1 %reduce-scatter.2.cloned.1.call-done = f32[256,3072]{0,1:T(8,128)} async-done(((f32[2048,3072]{0,1:T(8,128)}), f32[256,3072]{0,1:T(8,128)}) %reduce-scatter.2.cloned.1.call-update) | async-done | bytes 3145744 | tf_op jit(solution)/shard_map/reduce_scatter | solution.py:98
  283.0 3.8 fusion.6
  289.5 14.9 %fusion = bf16[1,512,2048]{2,1,0:T(8,128)(2,1)} fusion(bf16[2048,3072]{1,0:T(8,128)(2,1)} %param.4, bf16[512,1024]{0,1:T(8,128)(2,1)} %bitcast.87, bf16[512,1024]{0,1:T(8,128)(2,1)} %bitcast.89, bf16[512,1024]{0,1:T(8,128)(2,1)} %bitcast.92), kind=kOutput, calls=%fused_computation.8 | convolution fusion | flops 6452936704 | bytes 17825792 | tf_op jit(solution)/shard_map/dot_general | solution.py:94
  304.5 198.1 %all-gather.11.cloned.1.call-done = f32[1024,3072]{0,1:T(8,128)} async-done(((f32[256,3072]{0,1:T(8,128)}), f32[1024,3072]{0,1:T(8,128)}) %all-gather.11.cloned.1.call-update) | async-done | bytes 12582928 | tf_op jit(solution)/shard_map/all_gather | solution.py:106
  502.6 15.5 %reshape.171 = f32[4,256,3072]{1,0,2:T(4,128)} reshape(f32[1024,3072]{0,1:T(8,128)} %all-gather.11.cloned.1.call-done) | data formatting | bytes 25165824 | tf_op jit(solution)/shard_map/all_gather | solution.py:106
  518.1 19.5 %reduce_sum.29 = f32[256,3072]{0,1:T(8,128)} reduce(f32[4,256,3072]{1,0,2:T(4,128)} %reshape.171, f32[]{:T(128)} %constant.7.clone.1), dimensions={0}, to_apply=%region_3.4 | reduce | flops 2359296 | bytes 15728644 | tf_op jit(solution)/shard_map/reduce_sum | solution.py:106
  537.7 3.9 broadcast_multiply_fusion
  541.6 3.5 copy.44
  (60 shorter events, 15.6 us)
Async XLA Ops:
  7.2 2.8 copy-start
  7.2 60.6 %all-gather.9.cloned.1.call-start = ((), (), s32[]{:S(2)}) async-start(), calls=%async_computation.3 | async-start | bytes 4718592 | tf_op jit(solution)/shard_map/all_gather | solution.py:46
  24.1 3.0 copy-start.3
  26.0 1.0 copy-start.6
  28.3 78.0 %all-gather.7.cloned.1.call-start = ((), (), s32[]{:S(2)}) async-start(), calls=%async_computation.2 | async-start | bytes 4718592 | tf_op jit(solution)/shard_map/all_gather | solution.py:45
  35.8 247.2 %reduce-scatter.2.cloned.1.call-start = ((), (), s32[]{:S(2)}) async-start(), calls=%async_computation.1 | async-start | bytes 28311552 | tf_op jit(solution)/shard_map/reduce_scatter | solution.py:98
  36.1 2.8 copy-start.4
  36.1 2.8 copy-start.15
  40.4 4.9 copy-start.2
  40.4 2.0 copy-start.9
  42.5 2.9 copy-start.7
  67.8 2.9 copy-start.12
  67.8 3.1 copy-start.16
  70.9 2.2 copy-start.11
  106.3 2.9 copy-start.8
  106.3 3.2 copy-start.10
  109.5 1.2 copy-start.13
  109.5 2.1 copy-start.17
  109.5 2.1 copy-start.18
  110.7 1.0 copy-start.19
  126.8 375.8 %all-gather.11.cloned.1.call-start = ((), (), s32[]{:S(2)}) async-start(), calls=%async_computation.4 | async-start | bytes 15728640 | tf_op jit(solution)/shard_map/all_gather | solution.py:106
  283.0 3.8 copy-start.5
  283.0 3.8 copy-start.14
  537.7 7.4 %copy-start.1 = (bf16[1,512,2048]{2,1,0:T(8,128)(2,1)S(1)}, bf16[1,512,2048]{2,1,0:T(8,128)(2,1)}, u32[]{:S(2)}) copy-start(bf16[1,512,2048]{2,1,0:T(8,128)(2,1)} %param.3) | copy-start | bytes 6291460
Sparse Core Ops, SparseCore 0:
  28.5 39.3 all-gather.8
  69.7 36.5 all-gather.6
  126.9 156.0 reduce-scatter.1
  284.4 218.1 all-gather.10
